TPU v7x, 128 devices: a whole 4x4x4 slice. The times are simulated.
128 devices in a mesh: dp: 32 (over x, z, core), tensor: 4 (over y).
Axes of the slice: x: 4, y: 4, z: 4, core: 2. Of those that a mesh axis runs over, the one named last changes fastest.
Arguments:
- hidden_in: bfloat16 [32768, 768], P('dp'), may hold values from -6 to 6
- segments: int32 [32768], P('dp'), may hold values from 0 to 63, as said below
- positions: int32 [32768], P('dp'), may hold values from 0 to 1023, as said below
- first_gain: float32 [768], replicated, may hold values from 0.1 to 1.9
- first_shift: float32 [768], replicated, may hold values from -2 to 2
- heads_weight: bfloat16 [768, 2304], P(None, 'tensor'), may hold values from -0.21875 to 0.21875
- heads_bias: float32 [2304], P('tensor'), may hold values from -2 to 2
- dense_weight: bfloat16 [768, 768], P('tensor'), may hold values from -0.875 to 0.875
- dense_bias: float32 [768], replicated, may hold values from -3 to 3
- second_gain: float32 [768], replicated, may hold values from 0.1 to 1.9
- second_shift: float32 [768], replicated, may hold values from -2 to 2
- expand_weight: bfloat16 [768, 3072], P(None, 'tensor'), may hold values from -0.21875 to 0.21875
- expand_bias: float32 [3072], P('tensor'), may hold values from -3 to 3
- shrink_weight: bfloat16 [3072, 768], P('tensor'), may hold values from -0.109375 to 0.109375
- shrink_bias: float32 [768], replicated, may hold values from -3 to 3
- cotangent: bfloat16 [32768, 768], P('dp'), may hold values from -6 to 6
Outputs:
- hidden_out: bfloat16 [32768, 768], P('dp')
- hidden_gradient: bfloat16 [32768, 768], P('dp')
- first_gain_gradient: float32 [768], replicated
- first_shift_gradient: float32 [768], replicated
- heads_weight_gradient: float32 [768, 2304], P(None, 'tensor')
- heads_bias_gradient: float32 [2304], P('tensor')
- dense_weight_gradient: float32 [768, 768], P('tensor')
- dense_bias_gradient: float32 [768], replicated
- second_gain_gradient: float32 [768], replicated
- second_shift_gradient: float32 [768], replicated
- expand_weight_gradient: float32 [768, 3072], P(None, 'tensor')
- expand_bias_gradient: float32 [3072], P('tensor')
- shrink_weight_gradient: float32 [3072, 768], P('tensor')
- shrink_bias_gradient: float32 [768], replicated
Inputs may be any that keep to these rules, and one draw needn't show every extreme that they name: `segments`: each sequence s of 1024 tokens (rows s * 1024 to s * 1024 + 1023) holds 2 documents numbered s * 2 to s * 2 + 1 in order, segment numbers never falling; each document has 1024 // 2 - 2 * (128) tokens or more. Within a document positions rise by one from token to token; the first document of each sequence starts at 0; the last document of the first sequence ends at the largest position.
All inputs are finite; a program needn't handle non-finite values.
Results may differ from a plain program's by a relative error of at most 0.012.
The roundings to bfloat16 on the way count: a program that leaves them out, or rounds other values in their place, can miss the bound.
Values sent between devices are 32-bit elements; how exact they have to be, the bound alone decides.
No kernel may reach another device: no remote copies, remote signals or barrier semaphores. Data moves between devices by JAX's collectives and lax.ppermute only.
A program may use at most 128 MiB of HBM per device.

v0:
```python
import math

import jax
import jax.numpy as jnp
from jax import lax
from jax.sharding import PartitionSpec as P

HD = 64
ROT = 16


epsilon = 1e-05
rotary_base = 10000.0
block_limit = 512


def contract(pattern, left_op, right_op):
    return jnp.einsum(pattern, left_op, right_op, preferred_element_type=jnp.float32)


def layer_norm(wide_input):
    center = wide_input - jnp.mean(wide_input, axis=-1, keepdims=True)
    norm_scale = lax.rsqrt(jnp.mean(center * center, axis=-1, keepdims=True) + epsilon)
    return (center * norm_scale, norm_scale)


def norm_backward(upstream, normed, norm_scale, gain_row):
    scaled = upstream * gain_row
    return norm_scale * (
        scaled
        - jnp.mean(scaled, axis=-1, keepdims=True)
        - normed * jnp.mean(scaled * normed, axis=-1, keepdims=True)
    )


def gelu_value(hidden_pre):
    return hidden_pre * 0.5 * (1.0 + lax.erf(hidden_pre * (1.0 / math.sqrt(2.0))))


def gelu_slope(hidden_pre):
    return 0.5 * (1.0 + lax.erf(hidden_pre * (1.0 / math.sqrt(2.0)))) + hidden_pre * jnp.exp(
        -0.5 * hidden_pre * hidden_pre
    ) * (1.0 / math.sqrt(2.0 * math.pi))


def rotary_tables(seq_positions):
    half_rot = ROT // 2
    frequency = rotary_base ** (jnp.arange(half_rot).astype(jnp.float32) * (-2.0 / ROT))
    angles = seq_positions.astype(jnp.float32)[:, None] * frequency[None, :]
    angles = jnp.concatenate([angles, angles], axis=1)
    return (jnp.cos(angles), jnp.sin(angles))


def half_turn(front_dims):
    half_rot = ROT // 2
    return jnp.concatenate([-front_dims[..., half_rot:], front_dims[..., :half_rot]], axis=-1)


def rotate_forward(vectors, cosine, sine_table):
    front_dims = vectors[..., :ROT]
    turned = front_dims * cosine[:, None, :] + half_turn(front_dims) * sine_table[:, None, :]
    return jnp.concatenate([turned, vectors[..., ROT:]], axis=-1)


def rotate_backward(upstream, cosine, sine_table):
    front_dims = upstream[..., :ROT]
    turned = front_dims * cosine[:, None, :] - half_turn(front_dims * sine_table[:, None, :])
    return jnp.concatenate([turned, upstream[..., ROT:]], axis=-1)


def mask_block(seq_segments, first_row, last_row):
    token_index = jnp.arange(last_row)
    causal_ok = token_index[first_row:last_row, None] >= token_index[None, :]
    same_doc = seq_segments[first_row:last_row, None] == seq_segments[None, :last_row]
    return causal_ok & same_doc


def block_scores(queries, key_rows, seq_segments, first_row, last_row):
    scores = contract("hqd,hkd->hqk", queries[:, first_row:last_row], key_rows[:, :last_row]) * (
        1.0 / math.sqrt(HD)
    )
    return jnp.where(mask_block(seq_segments, first_row, last_row)[None], scores, -1e30)


def attend_forward(queries, key_rows, value_rows, seq_segments):
    row_count = queries.shape[1]
    block_size = min(row_count, block_limit)
    context_parts = []
    logsum_parts = []
    for first_row in range(0, row_count, block_size):
        last_row = first_row + block_size
        scores = block_scores(queries, key_rows, seq_segments, first_row, last_row)
        row_max = jnp.max(scores, axis=-1, keepdims=True)
        weights = jnp.exp(scores - row_max)
        row_total = jnp.sum(weights, axis=-1, keepdims=True)
        weights_low = (weights / row_total).astype(jnp.bfloat16)
        context_parts.append(
            contract("hqk,hkd->hqd", weights_low, value_rows[:, :last_row]).astype(jnp.bfloat16)
        )
        logsum_parts.append((row_max + jnp.log(row_total))[..., 0])
    return (jnp.concatenate(context_parts, axis=1), jnp.concatenate(logsum_parts, axis=1))


def attend_backward(queries, key_rows, value_rows, contexts, logsum, context_grad, seq_segments):
    row_count = queries.shape[1]
    block_size = min(row_count, block_limit)
    query_parts = []
    key_grad = jnp.zeros(key_rows.shape, jnp.float32)
    value_grad = jnp.zeros(value_rows.shape, jnp.float32)
    for first_row in range(0, row_count, block_size):
        last_row = first_row + block_size
        scores = block_scores(queries, key_rows, seq_segments, first_row, last_row)
        probs_back = jnp.exp(scores - logsum[:, first_row:last_row, None])
        probs_low = probs_back.astype(jnp.bfloat16)
        grad_block = context_grad[:, first_row:last_row]
        value_grad = value_grad.at[:, :last_row].add(
            contract("hqk,hqd->hkd", probs_low, grad_block)
        )
        prob_grad = contract("hqd,hkd->hqk", grad_block, value_rows[:, :last_row])
        row_inner = jnp.sum(
            grad_block.astype(jnp.float32) * contexts[:, first_row:last_row].astype(jnp.float32),
            axis=-1,
            keepdims=True,
        )
        score_grad = (probs_back * (prob_grad - row_inner) * (1.0 / math.sqrt(HD))).astype(
            jnp.bfloat16
        )
        query_parts.append(contract("hqk,hkd->hqd", score_grad, key_rows[:, :last_row]))
        key_grad = key_grad.at[:, :last_row].add(
            contract("hqk,hqd->hkd", score_grad, queries[:, first_row:last_row])
        )
    return (jnp.concatenate(query_parts, axis=1), key_grad, value_grad)


def on_device(
    hidden_in,
    segments,
    positions,
    first_gain,
    first_shift,
    heads_weight,
    heads_bias,
    dense_weight,
    dense_bias,
    second_gain,
    second_shift,
    expand_weight,
    expand_bias,
    shrink_weight,
    shrink_bias,
    cotangent,
):
    row_count = hidden_in.shape[0]
    head_count = heads_weight.shape[1] // (3 * HD)
    wide_input = hidden_in.astype(jnp.float32)
    normed, norm_scale = layer_norm(wide_input)
    first_input = (normed * first_gain + first_shift).astype(jnp.bfloat16)
    second_input = (normed * second_gain + second_shift).astype(jnp.bfloat16)
    mixed_rows = (
        jnp.dot(first_input, heads_weight, preferred_element_type=jnp.float32) + heads_bias
    ).reshape(row_count, head_count, 3, HD)
    cosine, sine_table = rotary_tables(positions)
    queries = (
        rotate_forward(mixed_rows[:, :, 0], cosine, sine_table)
        .astype(jnp.bfloat16)
        .transpose(1, 0, 2)
    )
    key_rows = (
        rotate_forward(mixed_rows[:, :, 1], cosine, sine_table)
        .astype(jnp.bfloat16)
        .transpose(1, 0, 2)
    )
    value_rows = mixed_rows[:, :, 2].astype(jnp.bfloat16).transpose(1, 0, 2)
    contexts, logsum = attend_forward(queries, key_rows, value_rows, segments)
    context_rows = contexts.transpose(1, 0, 2).reshape(row_count, head_count * HD)
    hidden_pre = (
        jnp.dot(second_input, expand_weight, preferred_element_type=jnp.float32) + expand_bias
    )
    activated = gelu_value(hidden_pre).astype(jnp.bfloat16)
    branch_part = jnp.dot(context_rows, dense_weight, preferred_element_type=jnp.float32) + jnp.dot(
        activated, shrink_weight, preferred_element_type=jnp.float32
    )
    branch = lax.psum(branch_part, "tensor")
    hidden_out = (wide_input + branch + dense_bias + shrink_bias).astype(jnp.bfloat16)
    grad_rows = cotangent.astype(jnp.float32)
    out_bias_grad = jnp.sum(grad_rows, axis=0)
    shrink_grad = jnp.dot(activated.T, cotangent, preferred_element_type=jnp.float32)
    pre_grad = jnp.dot(cotangent, shrink_weight.T, preferred_element_type=jnp.float32) * gelu_slope(
        hidden_pre
    )
    expand_bias_grad = jnp.sum(pre_grad, axis=0)
    pre_low = pre_grad.astype(jnp.bfloat16)
    expand_grad = jnp.dot(second_input.T, pre_low, preferred_element_type=jnp.float32)
    dense_grad = jnp.dot(context_rows.T, cotangent, preferred_element_type=jnp.float32)
    context_grad = jnp.dot(cotangent, dense_weight.T, preferred_element_type=jnp.float32).astype(
        jnp.bfloat16
    )
    context_grad = context_grad.reshape(row_count, head_count, HD).transpose(1, 0, 2)
    query_grad, key_grad, value_grad = attend_backward(
        queries, key_rows, value_rows, contexts, logsum, context_grad, segments
    )
    query_grad = rotate_backward(query_grad.transpose(1, 0, 2), cosine, sine_table)
    key_grad = rotate_backward(key_grad.transpose(1, 0, 2), cosine, sine_table)
    mixed_grad = jnp.stack([query_grad, key_grad, value_grad.transpose(1, 0, 2)], axis=2).reshape(
        row_count, head_count * 3 * HD
    )
    heads_bias_grad = jnp.sum(mixed_grad, axis=0)
    mixed_low = mixed_grad.astype(jnp.bfloat16)
    heads_grad = jnp.dot(first_input.T, mixed_low, preferred_element_type=jnp.float32)
    first_up = jnp.dot(mixed_low, heads_weight.T, preferred_element_type=jnp.float32)
    second_up = jnp.dot(pre_low, expand_weight.T, preferred_element_type=jnp.float32)
    input_part = norm_backward(first_up, normed, norm_scale, first_gain) + norm_backward(
        second_up, normed, norm_scale, second_gain
    )
    norm_terms = jnp.stack(
        [
            jnp.sum(first_up * normed, axis=0),
            jnp.sum(first_up, axis=0),
            jnp.sum(second_up * normed, axis=0),
            jnp.sum(second_up, axis=0),
        ]
    )
    norm_terms = lax.psum(norm_terms, ("dp", "tensor"))
    summed_input = lax.psum(input_part, "tensor")
    hidden_gradient = (grad_rows + summed_input).astype(jnp.bfloat16)
    (
        heads_grad,
        heads_bias_grad,
        dense_grad,
        out_bias_grad,
        expand_grad,
        expand_bias_grad,
        shrink_grad,
    ) = lax.psum(
        (
            heads_grad,
            heads_bias_grad,
            dense_grad,
            out_bias_grad,
            expand_grad,
            expand_bias_grad,
            shrink_grad,
        ),
        "dp",
    )
    return (
        hidden_out,
        hidden_gradient,
        norm_terms[0],
        norm_terms[1],
        heads_grad,
        heads_bias_grad,
        dense_grad,
        out_bias_grad,
        norm_terms[2],
        norm_terms[3],
        expand_grad,
        expand_bias_grad,
        shrink_grad,
        out_bias_grad,
    )


def solution(mesh):
    placed = (
        P("dp", None),
        P("dp"),
        P("dp"),
        P(),
        P(),
        P(None, "tensor"),
        P("tensor"),
        P("tensor", None),
        P(),
        P(),
        P(),
        P(None, "tensor"),
        P("tensor"),
        P("tensor", None),
        P(),
        P("dp", None),
    )
    return jax.shard_map(
        on_device,
        mesh=mesh,
        in_specs=placed,
        out_specs=(
            P("dp", None),
            P("dp", None),
            P(),
            P(),
            P(None, "tensor"),
            P("tensor"),
            P("tensor", None),
            P(),
            P(),
            P(),
            P(None, "tensor"),
            P("tensor"),
            P("tensor", None),
            P(),
        ),
        check_vma=False,
    )
```

profile of v0, /device:TPU:0, one launch (start us, length us, event | category | flops | bytes accessed | tf_op | source)
XLA Modules:
  0.0 334.0 jit_solution(16505256504611670689)
XLA Ops:
  7.3 1.8 convert_reduce_fusion
  9.1 2.0 fusion.25
  15.7 2.0 fusion
  17.7 2.1 fusion.56
  24.8 3.0 multiply_convert_fusion
  30.4 1.9 fusion.52
  34.2 1.9 multiply_convert_fusion.2
  36.2 3.4 %fusion.98 = (f32[768]{0:T(1024)}, bf16[1024,768]{1,0:T(8,128)(2,1)S(1)}) fusion(f32[1024,768]{1,0:T(8,128)S(1)} %get-tuple-element.128, f32[768]{0:T(1024)S(1)} %copy-done.27, bf16[1024,768]{1,0:T(8,128)(2,1)S(1)} %copy-done.3, bf16[768,768]{1,0:T(8,128)(2,1)S(1)} %copy-done.24), kind=kOutput, calls=%fused_computation.156 | convolution fusion | flops 1217395968 | bytes 7477248 | tf_op jit(solution)/shard_map/dot_general | solution.py:188
  39.6 1.4 fusion.60
  41.1 3.7 %fusion.23 = (f32[768]{0:T(1024)}, f32[1024]{0:T(1024)S(1)}, f32[1024]{0:T(1024)S(1)}, f32[768]{0:T(1024)}, f32[768]{0:T(1024)}, /*index=5*/f32[1024]{0:T(1024)S...) fusion(bf16[1024,768]{1,0:T(8,128)(2,1)S(1)} %copy-done.1, f32[1024]{0:T(1024)S(1)} %add_rsqrt_fusion, ...), kind=kOutput, calls=%fused_computation.34 | convolution fusion | flops 919331840 | bytes 9971712 | tf_op jit(solution)/shard_map/dot_general | solution.py:210
  46.3 2.3 convolution_add_fusion
  48.6 3.0 fusion.20
  51.7 2.8 fusion.102
  54.6 4.8 %fusion.103 = f32[768,768]{1,0:T(8,128)} fusion(bf16[1024,768]{1,0:T(8,128)(2,1)} %copy-done.32, bf16[1024,768]{1,0:T(8,128)(2,1)} %param.43), kind=kOutput, calls=%fused_computation.159 | convolution fusion | flops 1207959552 | bytes 5505024 | tf_op jit(solution)/shard_map/dot_general | solution.py:187
  59.4 2.6 fusion.92
  62.0 3.2 fusion.58
  65.2 1.6 fusion.42
  67.0 71.8 %psum.72 = f32[4,768]{1,0:T(4,128)S(1)} all-reduce(f32[4,768]{1,0:T(4,128)S(1)} %pad_maximum_fusion.3), channel_id=1, replica_groups=mesh['dp'=32,'tensor'=4] {'dp','tensor'}, use_global_device_ids=true, to_apply=%region_18.19 | all-reduce | flops 3072 | bytes 24576 | tf_op jit(solution)/shard_map/psum | solution.py:223
  139.4 43.5 %all-reduce.10.cloned.1.call-done = (f32[1024,768]{1,0:T(8,128)}, f32[1024,768]{1,0:T(8,128)}) async-done(((f32[1024,768]{1,0:T(8,128)}, f32[1024,768]{1,0:T(8,128)}), (f32[1024,768]{1,0:T(8,128)}, f32[1024,768]{1,0:T(8,128)})) %all-reduce.10.cloned.1.call-update) | async-done | bytes 6291472 | tf_op jit(solution)/shard_map/psum | solution.py:183
  182.9 4.2 %convert_reduce_fusion.1 = (f32[768]{0:T(1024)S(1)}, bf16[1024,768]{1,0:T(8,128)(2,1)}) fusion(bf16[1024,768]{1,0:T(8,128)(2,1)} %param.43, f32[1024,768]{1,0:T(8,128)} %get-tuple-element.104), kind=kLoop, calls=%fused_computation.11 | loop fusion | flops 3144960 | bytes 6294528 | tf_op jit(solution)/shard_map/reduce_sum | solution.py:186
  187.1 129.2 %all-reduce.2 = (f32[576]{0:T(1024)}, f32[768]{0:T(1024)S(1)}, f32[768]{0:T(1024)}) all-reduce(f32[576]{0:T(1024)S(1)} %reduce_sum.170, f32[768]{0:T(1024)S(1)} %get-tuple-element.107, f32[768]{0:T(1024)S(1)} %copy-done.17), channel_id=1, replica_groups=mesh['dp'=32,'tensor'=4] {'dp'}, use_global_device_ids=true, to_apply=%region_21.22 | all-reduce | flops 2112 | bytes 16896 | tf_op jit(solution)/shard_map/psum | solution.py:234
  316.3 3.5 %fusion.29 = bf16[1024,768]{1,0:T(8,128)(2,1)} fusion(f32[1024,768]{1,0:T(8,128)} %get-tuple-element.103, bf16[1024,768]{1,0:T(8,128)(2,1)S(1)} %copy-done.1, f32[768]{0:T(1024)S(1)} %copy-done.15, f32[768]{0:T(1024)S(1)} %copy-done.16), kind=kLoop, calls=%fused_computation.40 | loop fusion | flops 3932160 | bytes 6297600 | tf_op jit(solution)/shard_map/convert_element_type | solution.py:184
  320.5 3.1 copy.89
  324.4 1.4 copy.91
  (138 shorter events, 18.9 us)
Async XLA Ops:
  7.2 26.7 %copy-start = (bf16[768,768]{1,0:T(8,128)(2,1)S(1)}, bf16[768,768]{1,0:T(8,128)(2,1)}, u32[]{:S(2)}) copy-start(bf16[768,768]{1,0:T(8,128)(2,1)} %param.39) | copy-start | bytes 3538948
  7.2 4.0 %copy-start.1 = (bf16[1024,768]{1,0:T(8,128)(2,1)S(1)}, bf16[1024,768]{1,0:T(8,128)(2,1)}, u32[]{:S(2)}) copy-start(bf16[1024,768]{1,0:T(8,128)(2,1)} %param.28) | copy-start | bytes 4718596
  7.2 4.0 %copy-start.13 = (f32[768]{0:T(1024)S(1)}, f32[768]{0:T(1024)}, u32[]{:S(2)}) copy-start(f32[768]{0:T(1024)} %param.31) | copy-start | bytes 9220
  7.2 4.0 %copy-start.28 = (f32[768]{0:T(1024)S(1)}, f32[768]{0:T(1024)}, u32[]{:S(2)}) copy-start(f32[768]{0:T(1024)} %param.32) | copy-start | bytes 9220
  7.2 4.0 %copy-start.26 = (f32[576]{0:T(1024)S(1)}, f32[576]{0:T(1024)}, u32[]{:S(2)}) copy-start(f32[576]{0:T(1024)} %param.34) | copy-start | bytes 6916
  7.2 175.7 %all-reduce.10.cloned.1.call-start = ((), (), s32[]{:S(2)}) async-start(), calls=%async_computation.1 | async-start | bytes 12582912 | tf_op jit(solution)/shard_map/psum | solution.py:183
  7.3 3.9 %copy-start.25 = (bf16[768,576]{0,1:T(8,128)(2,1)S(1)}, bf16[768,576]{0,1:T(8,128)(2,1)}, u32[]{:S(2)}) copy-start(bf16[768,576]{0,1:T(8,128)(2,1)} %param.33) | copy-start | bytes 2654212
  34.2 6.8 %copy-start.8 = (bf16[1024,3,3,64]{0,3,2,1:T(8,128)(2,1)}, bf16[1024,3,3,64]{0,3,2,1:T(8,128)(2,1)S(1)}, u32[]{:S(2)}) copy-start(bf16[1024,3,3,64]{0,3,2,1:T(8,128)(2,1)S(1)} %copy.64) | copy-start | bytes 3538948
  34.2 2.0 copy-start.24
  36.2 8.7 %copy-start.32 = (bf16[1024,768]{1,0:T(8,128)(2,1)}, bf16[1024,768]{1,0:T(8,128)(2,1)S(1)}, u32[]{:S(2)}) copy-start(bf16[1024,768]{1,0:T(8,128)(2,1)S(1)} %get-tuple-element.127) | copy-start | bytes 4718596
  51.7 268.2 %all-reduce.8.cloned.1.call-start = ((), (), s32[]{:S(2)}) async-start(), calls=%async_computation | async-start | bytes 14155776 | tf_op jit(solution)/shard_map/psum | solution.py:234
  54.6 4.8 %copy-start.9 = (bf16[1024,3,3,64]{0,3,2,1:T(8,128)(2,1)S(1)}, bf16[1024,3,3,64]{0,3,2,1:T(8,128)(2,1)}, u32[]{:S(2)}) copy-start(bf16[1024,3,3,64]{0,3,2,1:T(8,128)(2,1)} %copy-done.8) | copy-start | bytes 3538948
  54.6 4.8 %copy-start.29 = (f32[768]{0:T(1024)S(1)}, f32[768]{0:T(1024)}, u32[]{:S(2)}) copy-start(f32[768]{0:T(1024)} %param.32) | copy-start | bytes 9220
  59.4 2.6 copy-start.31
  59.4 2.6 copy-start.34
  65.2 1.7 copy-start.19
  65.2 1.8 copy-start.18
  182.9 4.2 %copy-start.17 = (f32[768]{0:T(1024)S(1)}, f32[768]{0:T(1024)}, u32[]{:S(2)}) copy-start(f32[768]{0:T(1024)} %get-tuple-element.135) | copy-start | bytes 9220
  182.9 133.4 %copy-start.15 = (f32[768]{0:T(1024)S(1)}, f32[768]{0:T(1024)}, u32[]{:S(2)}) copy-start(f32[768]{0:T(1024)} %param.42) | copy-start | bytes 9220
  182.9 133.4 %copy-start.16 = (f32[768]{0:T(1024)S(1)}, f32[768]{0:T(1024)}, u32[]{:S(2)}) copy-start(f32[768]{0:T(1024)} %param.36) | copy-start | bytes 9220
  316.3 3.5 %copy-start.23 = (f32[768]{0:T(1024)}, f32[768]{0:T(1024)S(1)}, u32[]{:S(2)}) copy-start(f32[768]{0:T(1024)S(1)} %get-tuple-element.176) | copy-start | bytes 9220
  319.9 3.7 %copy-start.10 = (f32[192,768]{1,0:T(8,128)S(1)}, f32[192,768]{1,0:T(8,128)}, u32[]{:S(2)}) copy-start(f32[192,768]{1,0:T(8,128)} %get-tuple-element.175) | copy-start | bytes 1769476
  319.9 4.5 %copy-start.7 = (f32[768,768]{1,0:T(8,128)S(1)}, f32[768,768]{1,0:T(8,128)}, u32[]{:S(2)}) copy-start(f32[768,768]{1,0:T(8,128)} %get-tuple-element.179) | copy-start | bytes 7077892
  323.6 2.2 copy-start.6
  (13 other events, 15.2 us)
Sparse Core Ops, SparseCore 0:
  51.8 131.0 all-reduce.9
  187.9 118.3 all-reduce.7
where the time goes:
time: 334 us
  blocking collectives  201 us (60%)
  matrix products  43.8 us (13%)
  waiting for transfers between devices  43.6 us (13%)
  other arithmetic  20.4 us (6%)
  between operations  14.7 us (4%)
  local copies, waits for them, and re-layouts  10.5 us (3%)
    psum x1, blocking collectives, on_device(): lax.psum((heads_grad, heads_bias_grad, dense_grad, out_bias_grad, expand_...  129 us
    psum x1, blocking collectives, on_device(): norm_terms = lax.psum(norm_terms, ('dp', 'tensor'))  71.8 us
    psum x1, waiting for transfers between devices, on_device(): branch = lax.psum(branch_part, 'tensor')  43.5 us
    dot_general x12, matrix products, contract(): jnp.einsum(pattern, left_op, right_op, preferred_element_type=jnp.float32)  14.1 us
    unnamed x75, local copies, waits for them, and re-layouts  9.24 us
  transfers between devices with their start and end apart: 2, of which 1 were waited for; matrix products, arithmetic and copies ran while one was open for 7% of the time, Pallas kernels for 0%

commit v1 on v0

--- a/solution.py
+++ b/solution.py
@@ -130,6 +130,123 @@
             contract("hqk,hqd->hkd", score_grad, queries[:, first_row:last_row])
         )
     return (jnp.concatenate(query_parts, axis=1), key_grad, value_grad)
+
+
+N_DP = 32
+N_TENSOR = 4
+
+
+def pair_list(partner):
+    pairs = []
+    for row in range(N_DP):
+        for col in range(N_TENSOR):
+            to_row, to_col = partner(row, col)
+            pairs.append((row * N_TENSOR + col, to_row * N_TENSOR + to_col))
+    return pairs
+
+
+def swap(values, masks, axis):
+    if axis == "tensor":
+        pairs = pair_list(lambda row, col: (row, col ^ masks[row & 1]))
+    else:
+        pairs = pair_list(lambda row, col: (row ^ masks[row & 1], col))
+    return lax.ppermute(values, ("dp", "tensor"), pairs)
+
+
+def half_of(values, which, axis=0):
+    size = values.shape[axis] // 2
+    return lax.dynamic_slice_in_dim(values, which * size, size, axis)
+
+
+def joined(which, own, other, axis=0):
+    return jnp.where(
+        which == 0,
+        jnp.concatenate([own, other], axis=axis),
+        jnp.concatenate([other, own], axis=axis),
+    )
+
+
+def tensor_phases():
+    core = lax.axis_index("dp") & 1
+    place = lax.axis_index("tensor")
+    low, high = place & 1, place >> 1
+    return [
+        ((1, 3), jnp.where(core == 0, low ^ high, high), 0),
+        ((3, 1), jnp.where(core == 0, high, low), 0),
+    ]
+
+
+def dp_phases(orders):
+    index = lax.axis_index("dp")
+    core = index & 1
+    bit = [(index >> place) & 1 for place in range(5)]
+
+    def keeps(order):
+        seen, keep = set(), []
+        for mask in order:
+            if mask == 2:
+                keep.append(bit[1] if 6 in seen else bit[1] ^ bit[2])
+            elif mask == 6:
+                keep.append(bit[2])
+            elif mask == 8:
+                keep.append(bit[3] if 24 in seen else bit[3] ^ bit[4])
+            else:
+                keep.append(bit[4])
+            seen.add(mask)
+        return keep
+
+    first, second = keeps(orders[0]), keeps(orders[1])
+    phases = [((1, 1), core, 1)]
+    for step in range(4):
+        masks = (orders[0][step], orders[1][step])
+        phases.append((masks, jnp.where(core == 0, first[step], second[step]), 0))
+    return phases
+
+
+def after(values, *earlier):
+    return lax.optimization_barrier((values, earlier))[0]
+
+
+class Exchange:
+    def __init__(self, phases, halve, axis_name):
+        self.axis = axis_name
+        steps = [("halve", p) for p in phases[:halve]] + [("sum", p) for p in phases[halve:]]
+        self.steps = steps + [("join", p) for p in phases[:halve][::-1]]
+        self.values = None
+        self.flying = None
+
+    def put(self, values):
+        self.values = values
+        return self
+
+    def put_halves(self, own, other):
+        self.values = own
+        self.flying = swap(other, self.steps[0][1][0], self.axis)
+        return self
+
+    def send(self):
+        kind, (masks, keep, split) = self.steps[0]
+        outgoing = half_of(self.values, 1 - keep, split) if kind == "halve" else self.values
+        self.flying = swap(outgoing, masks, self.axis)
+        if kind == "halve":
+            self.values = half_of(self.values, keep, split)
+        return self
+
+    def land(self, *earlier):
+        kind, (masks, keep, split) = self.steps.pop(0)
+        arrived = after(self.flying, *earlier) if earlier else self.flying
+        if kind == "join":
+            self.values = joined(keep, self.values, arrived, split)
+        else:
+            self.values = self.values + arrived
+        if self.steps:
+            self.send()
+        return self.values
+
+    def finish(self):
+        while self.steps:
+            self.land()
+        return self.values
 
 
 def on_device(
@@ -150,8 +267,18 @@
     shrink_bias,
     cotangent,
 ):
-    row_count = hidden_in.shape[0]
-    head_count = heads_weight.shape[1] // (3 * HD)
+    row_count, width = hidden_in.shape
+    columns = heads_weight.shape[1]
+    head_count = columns // (3 * HD)
+    units = expand_weight.shape[1]
+    context_width = head_count * HD
+    half = row_count // 2
+    core = lax.axis_index("dp") & 1
+    y_phases = tensor_phases()
+    early_phases = dp_phases(((8, 2, 24, 6), (2, 8, 6, 24)))
+    late_phases = dp_phases(((24, 6, 8, 2), (6, 24, 2, 8)))
+    cosine, sine_table = rotary_tables(positions)
+
     wide_input = hidden_in.astype(jnp.float32)
     normed, norm_scale = layer_norm(wide_input)
     first_input = (normed * first_gain + first_shift).astype(jnp.bfloat16)
@@ -159,7 +286,6 @@
     mixed_rows = (
         jnp.dot(first_input, heads_weight, preferred_element_type=jnp.float32) + heads_bias
     ).reshape(row_count, head_count, 3, HD)
-    cosine, sine_table = rotary_tables(positions)
     queries = (
         rotate_forward(mixed_rows[:, :, 0], cosine, sine_table)
         .astype(jnp.bfloat16)
@@ -172,91 +298,131 @@
     )
     value_rows = mixed_rows[:, :, 2].astype(jnp.bfloat16).transpose(1, 0, 2)
     contexts, logsum = attend_forward(queries, key_rows, value_rows, segments)
-    context_rows = contexts.transpose(1, 0, 2).reshape(row_count, head_count * HD)
+    context_rows = contexts.transpose(1, 0, 2).reshape(row_count, context_width)
     hidden_pre = (
         jnp.dot(second_input, expand_weight, preferred_element_type=jnp.float32) + expand_bias
     )
     activated = gelu_value(hidden_pre).astype(jnp.bfloat16)
-    branch_part = jnp.dot(context_rows, dense_weight, preferred_element_type=jnp.float32) + jnp.dot(
-        activated, shrink_weight, preferred_element_type=jnp.float32
-    )
-    branch = lax.psum(branch_part, "tensor")
-    hidden_out = (wide_input + branch + dense_bias + shrink_bias).astype(jnp.bfloat16)
-    grad_rows = cotangent.astype(jnp.float32)
-    out_bias_grad = jnp.sum(grad_rows, axis=0)
-    shrink_grad = jnp.dot(activated.T, cotangent, preferred_element_type=jnp.float32)
-    pre_grad = jnp.dot(cotangent, shrink_weight.T, preferred_element_type=jnp.float32) * gelu_slope(
+
+    keep = y_phases[0][1]
+
+    def branch_rows(which):
+        part = jnp.dot(
+            half_of(context_rows, which), dense_weight, preferred_element_type=jnp.float32
+        )
+        return part + jnp.dot(
+            half_of(activated, which), shrink_weight, preferred_element_type=jnp.float32
+        )
+
+    part_other = branch_rows(1 - keep)
+    part_own = branch_rows(keep)
+    out = Exchange(y_phases, 1, "tensor").put_halves(part_own, part_other)
+
+    upstream = after(cotangent, part_own)
+    pre_grad = jnp.dot(upstream, shrink_weight.T, preferred_element_type=jnp.float32) * gelu_slope(
         hidden_pre
     )
-    expand_bias_grad = jnp.sum(pre_grad, axis=0)
     pre_low = pre_grad.astype(jnp.bfloat16)
-    expand_grad = jnp.dot(second_input.T, pre_low, preferred_element_type=jnp.float32)
-    dense_grad = jnp.dot(context_rows.T, cotangent, preferred_element_type=jnp.float32)
-    context_grad = jnp.dot(cotangent, dense_weight.T, preferred_element_type=jnp.float32).astype(
-        jnp.bfloat16
-    )
+    ones = (jnp.arange(32) == 0).astype(jnp.bfloat16)[None, :] * jnp.ones(
+        (row_count, 1), jnp.bfloat16
+    )
+    output_side = jnp.concatenate([activated, context_rows, ones], axis=1)
+    input_side = jnp.concatenate([second_input, ones], axis=1)
+
+    def early_columns(which):
+        parts = [
+            jnp.dot(left.T, half_of(right, which, 1), preferred_element_type=jnp.float32)
+            for left, right in ((output_side, upstream), (input_side, pre_low))
+        ]
+        return jnp.concatenate(parts, axis=0)
+
+    early_other = early_columns(1 - core)
+    early_own = early_columns(core)
+    early = Exchange(early_phases, 3, "dp").put_halves(early_own, early_other)
+    landed = [out.land(early_own)]
+
+    context_grad = jnp.dot(
+        after(cotangent, landed), dense_weight.T, preferred_element_type=jnp.float32
+    ).astype(jnp.bfloat16)
     context_grad = context_grad.reshape(row_count, head_count, HD).transpose(1, 0, 2)
+    landed = [early.land(context_grad)]
     query_grad, key_grad, value_grad = attend_backward(
-        queries, key_rows, value_rows, contexts, logsum, context_grad, segments
-    )
+        queries, key_rows, value_rows, contexts, logsum, after(context_grad, landed), segments
+    )
+    landed = [out.land(query_grad), early.land(query_grad)]
+    query_grad = after(query_grad, landed)
     query_grad = rotate_backward(query_grad.transpose(1, 0, 2), cosine, sine_table)
     key_grad = rotate_backward(key_grad.transpose(1, 0, 2), cosine, sine_table)
     mixed_grad = jnp.stack([query_grad, key_grad, value_grad.transpose(1, 0, 2)], axis=2).reshape(
-        row_count, head_count * 3 * HD
-    )
-    heads_bias_grad = jnp.sum(mixed_grad, axis=0)
+        row_count, columns
+    )
     mixed_low = mixed_grad.astype(jnp.bfloat16)
-    heads_grad = jnp.dot(first_input.T, mixed_low, preferred_element_type=jnp.float32)
     first_up = jnp.dot(mixed_low, heads_weight.T, preferred_element_type=jnp.float32)
     second_up = jnp.dot(pre_low, expand_weight.T, preferred_element_type=jnp.float32)
     input_part = norm_backward(first_up, normed, norm_scale, first_gain) + norm_backward(
         second_up, normed, norm_scale, second_gain
     )
-    norm_terms = jnp.stack(
+    back = Exchange(y_phases, 1, "tensor").put(input_part).send()
+
+    sums = jnp.stack(
         [
             jnp.sum(first_up * normed, axis=0),
             jnp.sum(first_up, axis=0),
             jnp.sum(second_up * normed, axis=0),
             jnp.sum(second_up, axis=0),
+            jnp.pad(jnp.sum(mixed_grad, axis=0), (0, width - columns)),
         ]
     )
-    norm_terms = lax.psum(norm_terms, ("dp", "tensor"))
-    summed_input = lax.psum(input_part, "tensor")
-    hidden_gradient = (grad_rows + summed_input).astype(jnp.bfloat16)
-    (
-        heads_grad,
-        heads_bias_grad,
-        dense_grad,
-        out_bias_grad,
-        expand_grad,
-        expand_bias_grad,
-        shrink_grad,
-    ) = lax.psum(
-        (
-            heads_grad,
-            heads_bias_grad,
-            dense_grad,
-            out_bias_grad,
-            expand_grad,
-            expand_bias_grad,
-            shrink_grad,
-        ),
-        "dp",
-    )
+    sums = jnp.pad(sums, ((0, 59), (0, 0)))
+
+    def late_columns(which):
+        part = jnp.dot(
+            mixed_low.T, half_of(first_input, which, 1), preferred_element_type=jnp.float32
+        )
+        return jnp.concatenate([part, half_of(sums, which, 1)], axis=0)
+
+    late_other = late_columns(1 - core)
+    late_own = late_columns(core)
+    late = Exchange(late_phases, 3, "dp").put_halves(late_own, late_other)
+    landed = early.land(late_own)
+    landed = late.land(landed)
+    landed = out.land(landed)
+    landed = late.land(landed)
+    landed = early.land(landed)
+    landed = back.land(landed)
+    landed = late.land(landed)
+    landed = early.land(landed)
+    landed = late.land(landed)
+    landed = late.land(landed)
+    landed = early.land(landed)
+    landed = back.land(landed)
+    landed = late.finish()
+    early.finish()
+    back.finish()
+
+    hidden_out = (wide_input + out.values + dense_bias + shrink_bias).astype(jnp.bfloat16)
+    hidden_gradient = (cotangent.astype(jnp.float32) + back.values).astype(jnp.bfloat16)
+    early, late = early.values, late.values
+    norm_terms = late[columns : columns + 8]
+    for mask in (1, 3):
+        norm_terms = norm_terms + swap(norm_terms, (mask, mask), "tensor")
+    dense_row = units + context_width
+    out_bias_grad = early[dense_row]
+    expand_row = dense_row + 32
     return (
         hidden_out,
         hidden_gradient,
         norm_terms[0],
         norm_terms[1],
-        heads_grad,
-        heads_bias_grad,
-        dense_grad,
+        late[:columns].T,
+        late[columns + 4, :columns],
+        early[units:dense_row],
         out_bias_grad,
         norm_terms[2],
         norm_terms[3],
-        expand_grad,
-        expand_bias_grad,
-        shrink_grad,
+        early[expand_row : expand_row + width],
+        early[expand_row + width],
+        early[:units],
         out_bias_grad,
     )
 

time: 334 us -> 267 us (0.80)
  the two profiles are of different devices: /device:TPU:0 before, /device:TPU:64 now
where the time goes in v1:
time: 267 us; the launch traced here: 262 us
  waiting for transfers between devices  97 us (36%)
  matrix products  55.7 us (21%)
  other arithmetic  54.9 us (21%)
  starting transfers between devices  29.2 us (11%)
  local copies, waits for them, and re-layouts  23.3 us (9%)
    ppermute x24, waiting for transfers between devices, swap(): return lax.ppermute(values, ('dp', 'tensor'), pairs)  97 us
    ppermute x24, starting transfers between devices, swap(): return lax.ppermute(values, ('dp', 'tensor'), pairs)  29.2 us
    dot_general x12, matrix products, contract(): jnp.einsum(pattern, left_op, right_op, preferred_element_type=jnp.float32)  17.9 us
    select_n x6, other arithmetic, joined(): jnp.where(which == 0, jnp.concatenate([own, other], axis=axis), jnp.conca...  14.6 us
    add x14, other arithmetic, land(): self.values = self.values + arrived  12.7 us
    unnamed x139, local copies, waits for them, and re-layouts  9.91 us
    dot_general x1, matrix products, on_device(): jnp.dot(pre_low, expand_weight.T, preferred_element_type=jnp.float32)  6.7 us
    dot_general x4, matrix products, early_columns(): jnp.dot(left.T, half_of(right, which, 1), preferred_element_type=jnp.floa...  6.67 us
  transfers between devices with their start and end apart: 24, of which 12 were waited for; matrix products, arithmetic and copies ran while one was open for 24% of the time, Pallas kernels for 0%

profile of v1, /device:TPU:64, one launch (start us, length us, event | category | flops | bytes accessed | tf_op | source)
XLA Modules:
  0.0 262.1 jit_solution(7213737972886456492)
XLA Ops:
  23.7 3.9 %fusion.60 = bf16[3,512,64]{1,2,0:T(8,128)(2,1)} fusion(f32[3,512,1024]{2,1,0:T(8,128)S(1)} %get-tuple-element.176, f32[3,512]{1,0:T(4,128)S(1)} %fusion, f32[3,512]{1,0:T(4,128)S(1)} %get-tuple-element.175, pred[512,1024]{1,0:T(8,128)(4,1)S(1)} %fusion.43, f32[1024,3,3,64]{0,3,2,1:T(8,128)} %bitcast.68), kind=kOutput, calls=%fused_computation.91 | convolution fusion | flops 209289216 | bytes 7417856 | tf_op jit(solution)/shard_map/hqk,hkd->hqd/dot_general | solution.py:18
  32.0 3.1 %multiply_convert_fusion.2 = (bf16[1024,768]{0,1:T(8,128)(2,1)S(1)}, f32[1024,768]{0,1:T(8,128)}) fusion(f32[768]{0:T(1024)S(1)} %copy-done.62, bf16[1024,768]{1,0:T(8,128)(2,1)S(1)} %copy-done.21, bf16[768,768]{1,0:T(8,128)(2,1)S(1)} %copy-done), kind=kOutput, calls=%fused_computation.51 | convolution fusion | flops 1212678144 | bytes 7474176 | tf_op jit(solution)/shard_map/dot_general | solution.py:303
  38.3 5.0 %fusion.34 = bf16[1024,768]{0,1:T(8,128)(2,1)S(1)} fusion(f32[1024,768]{0,1:T(8,128)} %get-tuple-element.180, bf16[1024,768]{1,0:T(8,128)(2,1)} %param.43, bf16[768,768]{1,0:T(8,128)(2,1)} %param.41, f32[768]{0:T(1024)} %param.40), kind=kOutput, calls=%fused_computation.44 | convolution fusion | flops 1216610304 | bytes 7474176 | tf_op jit(solution)/shard_map/dot_general | solution.py:322
  50.2 3.5 %convolution_add_fusion.1 = f32[512,768]{1,0:T(8,128)} fusion(f32[512,768]{1,0:T(8,128)S(1)} %fusion.83, bf16[768,768]{1,0:T(8,128)(2,1)} %param.41, bf16[1024,768]{0,1:T(8,128)(2,1)} %copy-done.63, s32[]{:T(128)S(6)} %select_n.137), kind=kOutput, calls=%fused_computation.82 | convolution fusion | flops 604372992 | bytes 5111812 | tf_op jit(solution)/shard_map/dot_general | solution.py:313
  56.7 3.0 %fusion.51 = f32[800,384]{1,0:T(8,128)S(1)} fusion(bf16[1024,768]{1,0:T(8,128)(2,1)} %get-tuple-element.148, bf16[800]{0:T(1024)(128)(2,1)} %pad.76.clone, bf16[1024,768]{0,1:T(8,128)(2,1)} %copy-done.66, s32[]{:T(128)S(6)} %select_n.138), kind=kOutput, calls=%fused_computation.81 | convolution fusion | flops 632422400 | bytes 3590148 | tf_op jit(solution)/shard_map/dot_general | solution.py:334
  61.0 13.4 %collective-permute-done = f32[512,768]{1,0:T(8,128)} collective-permute-done((f32[512,768]{1,0:T(8,128)}, f32[512,768]{1,0:T(8,128)}, u32[]{:S(2)}, u32[]{:S(2)}) %collective-permute-start) | collective-permute-done | bytes 1572896 | tf_op jit(solution)/shard_map/ppermute | solution.py:153
  76.0 3.1 %collective-permute-start.1 = (f32[512,768]{1,0:T(8,128)S(1)}, f32[512,768]{1,0:T(8,128)S(1)}, u32[]{:S(2)}, u32[]{:S(2)}) collective-permute-start(f32[512,768]{1,0:T(8,128)S(1)} %add.252), channel_id=1, source_target_pairs={{0,3},{1,2},{2,1},{3,0},{4,5},{5,4},{6,7},{7,6},{8,11},{9,10},{10,... | collective-permute-start | bytes 4718600 | tf_op jit(solution)/shard_map/ppermute | solution.py:153
  84.9 4.0 %multiply_convert_fusion = bf16[3,512,1024]{2,1,0:T(8,128)(2,1)S(1)} fusion(f32[3,512,1024]{2,1,0:T(8,128)S(1)} %bitcast.62, f32[3,512]{1,0:T(4,128)S(1)} %get-tuple-element.133, f32[3,512]{1,0:T(4,128)S(1)} %log_add_fusion, pred[512,1024]{1,0:T(8,128)(4,1)S(1)} %copy-done.13, bf16[3,1024,64]{1,2,0:T(8,128)(2,1)S(1)} %bitcast.71, f32[1024,3,3,64]{0,3,2,1:T(8,128)} %bitcast.69), kind=kOutput, calls=%fused_computation | convolution fusion | flops 212336640 | bytes 10567680 | tf_op jit(solution)/shard_map/hqd,hkd->hqk/dot_general | solution.py:18
  92.8 8.9 %collective-permute-done.4 = f32[896,384]{1,0:T(8,128)S(1)} collective-permute-done((f32[896,384]{1,0:T(8,128)S(1)}, f32[896,384]{1,0:T(8,128)S(1)}, u32[]{:S(2)}, u32[]{:S(2)}) %collective-permute-start.4) | collective-permute-done | bytes 1376288 | tf_op jit(solution)/shard_map/ppermute | solution.py:153
  107.8 5.3 %collective-permute-done.6 = f32[448,384]{1,0:T(8,128)S(1)} collective-permute-done((f32[448,384]{1,0:T(8,128)S(1)}, f32[448,384]{1,0:T(8,128)S(1)}, u32[]{:S(2)}, u32[]{:S(2)}) %collective-permute-start.6) | collective-permute-done | bytes 688160 | tf_op jit(solution)/shard_map/ppermute | solution.py:153
  117.1 3.1 %fusion.132 = f32[1024,768]{1,0:T(8,128)} fusion(bf16[1024,576]{0,1:T(8,128)(2,1)S(1)} %bitcast.80, bf16[768,576]{0,1:T(8,128)(2,1)S(1)} %copy-done.60), kind=kOutput, calls=%fused_computation.222 | convolution fusion | flops 905969664 | bytes 5210112 | tf_op jit(solution)/shard_map/dot_general | solution.py:360
  120.3 6.7 %fusion.23 = (f32[1024]{0:T(1024)S(1)}, f32[768]{0:T(1024)S(1)}, f32[1024]{0:T(1024)S(1)}, f32[768]{0:T(1024)S(1)}, f32[768]{0:T(1024)S(1)}, /*index=5*/f32[1024...) fusion(bf16[1024,768]{1,0:T(8,128)(2,1)S(1)} %copy-done.3, f32[768]{0:T(1024)S(1)} %copy-done.45, ...), kind=kOutput, calls=%fused_computation.33 | convolution fusion | flops 1221321728 | bytes 10659840 | tf_op jit(solution)/shard_map/dot_general | solution.py:361
  133.1 5.5 %fusion.28 = (bf16[1024,768]{1,0:T(8,128)(2,1)}, f32[1024,768]{1,0:T(8,128)S(1)}) fusion(bf16[1024,768]{1,0:T(8,128)(2,1)S(1)} %copy-done.3, f32[768]{0:T(1024)S(1)} %copy-done.52, f32[768]{0:T(1024)S(1)} %copy-done.53, f32[512,768]{1,0:T(8,128)} %add.258, f32[512,768]{1,0:T(8,128)} %collective-permute-done.3, pred[]{:T(512)S(6)} %eq.86, ...), kind=kLoop, calls=%fused_computation.38 | loop fusion | flops 15728640 | bytes 15765505 | tf_op jit(solution)/shard_map/convert_element_type | solution.py:403
  141.6 3.0 %collective-permute-start.8 = (f32[448,384]{1,0:T(8,128)S(1)}, f32[448,384]{1,0:T(8,128)}, u32[]{:S(2)}, u32[]{:S(2)}) collective-permute-start(f32[448,384]{1,0:T(8,128)S(1)} %fusion.125), channel_id=1, source_target_pairs={{0,96},{1,97},{2,98},{3,99},{4,28},{5,29},{6,30},{7,31},{8,104},{9... | collective-permute-start | bytes 2064392 | tf_op jit(solution)/shard_map/ppermute | solution.py:153
  145.1 14.2 %collective-permute-done.9 = f32[320,384]{1,0:T(8,128)S(1)} collective-permute-done((f32[320,384]{1,0:T(8,128)}, f32[320,384]{1,0:T(8,128)S(1)}, u32[]{:S(2)}, u32[]{:S(2)}) %collective-permute-start.9) | collective-permute-done | bytes 491552 | tf_op jit(solution)/shard_map/ppermute | solution.py:153
  164.3 9.9 %collective-permute-done.12 = f32[160,384]{1,0:T(8,128)S(1)} collective-permute-done((f32[160,384]{1,0:T(8,128)S(1)}, f32[160,384]{1,0:T(8,128)S(1)}, u32[]{:S(2)}, u32[]{:S(2)}) %collective-permute-start.12) | collective-permute-done | bytes 245792 | tf_op jit(solution)/shard_map/ppermute | solution.py:153
  177.5 8.1 %collective-permute-done.14 = f32[160,384]{1,0:T(8,128)S(1)} collective-permute-done((f32[160,384]{1,0:T(8,128)S(1)}, f32[160,384]{1,0:T(8,128)S(1)}, u32[]{:S(2)}, u32[]{:S(2)}) %collective-permute-start.14) | collective-permute-done | bytes 245792 | tf_op jit(solution)/shard_map/ppermute | solution.py:153
  187.0 5.9 %collective-permute-done.15 = f32[160,384]{1,0:T(8,128)} collective-permute-done((f32[160,384]{1,0:T(8,128)}, f32[160,384]{1,0:T(8,128)}, u32[]{:S(2)}, u32[]{:S(2)}) %collective-permute-start.15) | collective-permute-done | bytes 245792 | tf_op jit(solution)/shard_map/ppermute | solution.py:153
  199.1 6.4 %collective-permute-done.17 = f32[160,384]{1,0:T(8,128)S(1)} collective-permute-done((f32[160,384]{1,0:T(8,128)}, f32[160,384]{1,0:T(8,128)S(1)}, u32[]{:S(2)}, u32[]{:S(2)}) %collective-permute-start.17) | collective-permute-done | bytes 245792 | tf_op jit(solution)/shard_map/ppermute | solution.py:153
  209.1 6.7 %collective-permute-done.22 = f32[896,384]{1,0:T(8,128)} collective-permute-done((f32[896,384]{1,0:T(8,128)}, f32[896,384]{1,0:T(8,128)}, u32[]{:S(2)}, u32[]{:S(2)}) %collective-permute-start.22) | collective-permute-done | bytes 1376288 | tf_op jit(solution)/shard_map/ppermute | solution.py:153
  215.8 4.4 %maximum_select_fusion.3 = f32[1792,384]{1,0:T(8,128)} fusion(f32[896,384]{1,0:T(8,128)} %collective-permute-done.22, f32[896,384]{1,0:T(8,128)} %maximum_select_fusion.5, pred[]{:T(512)S(6)} %eq.98), kind=kLoop, calls=%fused_computation.65 | loop fusion | flops 2064384 | bytes 5505025 | tf_op jit(solution)/shard_map/jit(_where)/select_n | solution.py:162
  230.5 14.3 %collective-permute-done.20 = f32[8,768]{1,0:T(8,128)S(1)} collective-permute-done((f32[8,768]{1,0:T(8,128)S(1)}, f32[8,768]{1,0:T(8,128)S(1)}, u32[]{:S(2)}, u32[]{:S(2)}) %collective-permute-start.20) | collective-permute-done | bytes 24608 | tf_op jit(solution)/shard_map/ppermute | solution.py:153
  246.9 3.0 %collective-permute-done.21 = f32[8,768]{1,0:T(8,128)S(1)} collective-permute-done((f32[8,768]{1,0:T(8,128)S(1)}, f32[8,768]{1,0:T(8,128)S(1)}, u32[]{:S(2)}, u32[]{:S(2)}) %collective-permute-start.21) | collective-permute-done | bytes 24608 | tf_op jit(solution)/shard_map/ppermute | solution.py:153
  252.3 5.1 %maximum_select_fusion = f32[1792,768]{1,0:T(8,128)S(1)} fusion(f32[1792,384]{1,0:T(8,128)} %collective-permute-done.23, f32[1792,384]{1,0:T(8,128)} %maximum_select_fusion.3, pred[]{:T(512)S(6)} %eq.42), kind=kLoop, calls=%fused_computation.7 | loop fusion | flops 4128768 | bytes 11010049 | tf_op jit(solution)/shard_map/jit(_where)/select_n | solution.py:162
  (289 shorter events, 110.5 us)
Async XLA Ops:
  48.3 31.5 %collective-permute-start.2 = (f32[1792,384]{1,0:T(8,128)}, f32[1792,384]{1,0:T(8,128)}, u32[]{:S(2)}, u32[]{:S(2)}) collective-permute-start(f32[1792,384]{1,0:T(8,128)} %pad_maximum_fusion.1), channel_id=1, source_target_pairs={{0,4},{1,5},{2,6},{3,7},{4,0},{5,1},{6,2},{7,3},{8,12},{9,13},{10,... | collective-permute-start | bytes 8257544 | tf_op jit(solution)/shard_map/ppermute | solution.py:153
  53.6 20.7 %collective-permute-start = (f32[512,768]{1,0:T(8,128)}, f32[512,768]{1,0:T(8,128)}, u32[]{:S(2)}, u32[]{:S(2)}) collective-permute-start(f32[512,768]{1,0:T(8,128)} %convolution_add_fusion.1), channel_id=1, source_target_pairs={{0,1},{1,0},{2,3},{3,2},{4,7},{5,6},{6,5},{7,4},{8,9},{9,8},{10,11... | collective-permute-start | bytes 4718600 | tf_op jit(solution)/shard_map/ppermute | solution.py:153
  76.0 30.4 %collective-permute-start.1 = (f32[512,768]{1,0:T(8,128)S(1)}, f32[512,768]{1,0:T(8,128)S(1)}, u32[]{:S(2)}, u32[]{:S(2)}) collective-permute-start(f32[512,768]{1,0:T(8,128)S(1)} %add.252), channel_id=1, source_target_pairs={{0,3},{1,2},{2,1},{3,0},{4,5},{5,4},{6,7},{7,6},{8,11},{9,10},{10,... | collective-permute-start | bytes 4718600 | tf_op jit(solution)/shard_map/ppermute | solution.py:153
  83.4 18.4 %collective-permute-start.4 = (f32[896,384]{1,0:T(8,128)S(1)}, f32[896,384]{1,0:T(8,128)S(1)}, u32[]{:S(2)}, u32[]{:S(2)}) collective-permute-start(f32[896,384]{1,0:T(8,128)S(1)} %get-tuple-element.144), channel_id=1, source_target_pairs={{0,32},{1,33},{2,34},{3,35},{4,12},{5,13},{6,14},{7,15},{8,40},{9,... | collective-permute-start | bytes 4128776 | tf_op jit(solution)/shard_map/ppermute | solution.py:153
  102.0 11.2 %collective-permute-start.6 = (f32[448,384]{1,0:T(8,128)S(1)}, f32[448,384]{1,0:T(8,128)S(1)}, u32[]{:S(2)}, u32[]{:S(2)}) collective-permute-start(f32[448,384]{1,0:T(8,128)S(1)} %constant_dynamic-slice_fusion.5), channel_id=1, source_target_pairs={{0,8},{1,9},{2,10},{3,11},{4,36},{5,37},{6,38},{7,39},{8,0},{9,1},... | collective-permute-start | bytes 2064392 | tf_op jit(solution)/shard_map/ppermute | solution.py:153
  107.7 24.3 %collective-permute-start.3 = (f32[512,768]{1,0:T(8,128)}, f32[512,768]{1,0:T(8,128)}, u32[]{:S(2)}, u32[]{:S(2)}) collective-permute-start(f32[512,768]{1,0:T(8,128)} %add.258), channel_id=1, source_target_pairs={{0,1},{1,0},{2,3},{3,2},{4,7},{5,6},{6,5},{7,4},{8,9},{9,8},{10,11... | collective-permute-start | bytes 4718600 | tf_op jit(solution)/shard_map/ppermute | solution.py:153
  128.3 2.6 %collective-permute-start.5 = (f32[640,384]{1,0:T(8,128)S(1)}, f32[640,384]{1,0:T(8,128)S(1)}, u32[]{:S(2)}, u32[]{:S(2)}) collective-permute-start(f32[640,384]{1,0:T(8,128)S(1)} %pad_maximum_fusion.7), channel_id=1, source_target_pairs={{0,4},{1,5},{2,6},{3,7},{4,0},{5,1},{6,2},{7,3},{8,12},{9,13},{10,... | collective-permute-start | bytes 2949128 | tf_op jit(solution)/shard_map/ppermute | solution.py:153
  141.5 21.2 %collective-permute-start.7 = (f32[512,768]{1,0:T(8,128)}, f32[512,768]{1,0:T(8,128)}, u32[]{:S(2)}, u32[]{:S(2)}) collective-permute-start(f32[512,768]{1,0:T(8,128)} %constant_dynamic-slice_fusion.3), channel_id=1, source_target_pairs={{0,1},{1,0},{2,3},{3,2},{4,7},{5,6},{6,5},{7,4},{8,9},{9,8},{10,11... | collective-permute-start | bytes 4718600 | tf_op jit(solution)/shard_map/ppermute | solution.py:153
  141.6 17.8 %collective-permute-start.8 = (f32[448,384]{1,0:T(8,128)S(1)}, f32[448,384]{1,0:T(8,128)}, u32[]{:S(2)}, u32[]{:S(2)}) collective-permute-start(f32[448,384]{1,0:T(8,128)S(1)} %fusion.125), channel_id=1, source_target_pairs={{0,96},{1,97},{2,98},{3,99},{4,28},{5,29},{6,30},{7,31},{8,104},{9... | collective-permute-start | bytes 2064392 | tf_op jit(solution)/shard_map/ppermute | solution.py:153
  144.6 14.6 %collective-permute-start.9 = (f32[320,384]{1,0:T(8,128)}, f32[320,384]{1,0:T(8,128)S(1)}, u32[]{:S(2)}, u32[]{:S(2)}) collective-permute-start(f32[320,384]{1,0:T(8,128)} %get-tuple-element.151), channel_id=1, source_target_pairs={{0,96},{1,97},{2,98},{3,99},{4,28},{5,29},{6,30},{7,31},{8,104},{9... | collective-permute-start | bytes 1474568 | tf_op jit(solution)/shard_map/ppermute | solution.py:153
  160.6 13.7 %collective-permute-start.11 = (f32[448,384]{1,0:T(8,128)S(1)}, f32[448,384]{1,0:T(8,128)S(1)}, u32[]{:S(2)}, u32[]{:S(2)}) collective-permute-start(f32[448,384]{1,0:T(8,128)S(1)} %add.277), channel_id=1, source_target_pairs={{0,24},{1,25},{2,26},{3,27},{4,100},{5,101},{6,102},{7,103},{8,16}... | collective-permute-start | bytes 2064392 | tf_op jit(solution)/shard_map/ppermute | solution.py:153
  160.7 13.5 %collective-permute-start.12 = (f32[160,384]{1,0:T(8,128)S(1)}, f32[160,384]{1,0:T(8,128)S(1)}, u32[]{:S(2)}, u32[]{:S(2)}) collective-permute-start(f32[160,384]{1,0:T(8,128)S(1)} %get-tuple-element.157), channel_id=1, source_target_pairs={{0,24},{1,25},{2,26},{3,27},{4,100},{5,101},{6,102},{7,103},{8,16}... | collective-permute-start | bytes 737288 | tf_op jit(solution)/shard_map/ppermute | solution.py:153
  174.4 20.3 %collective-permute-start.13 = (f32[448,384]{1,0:T(8,128)S(1)}, f32[448,384]{1,0:T(8,128)}, u32[]{:S(2)}, u32[]{:S(2)}) collective-permute-start(f32[448,384]{1,0:T(8,128)S(1)} %add.281), channel_id=1, source_target_pairs={{0,8},{1,9},{2,10},{3,11},{4,36},{5,37},{6,38},{7,39},{8,0},{9,1},... | collective-permute-start | bytes 2064392 | tf_op jit(solution)/shard_map/ppermute | solution.py:153
  177.3 8.4 %collective-permute-start.14 = (f32[160,384]{1,0:T(8,128)S(1)}, f32[160,384]{1,0:T(8,128)S(1)}, u32[]{:S(2)}, u32[]{:S(2)}) collective-permute-start(f32[160,384]{1,0:T(8,128)S(1)} %add.280), channel_id=1, source_target_pairs={{0,32},{1,33},{2,34},{3,35},{4,12},{5,13},{6,14},{7,15},{8,40},{9,... | collective-permute-start | bytes 737288 | tf_op jit(solution)/shard_map/ppermute | solution.py:153
  186.4 6.5 %collective-permute-start.15 = (f32[160,384]{1,0:T(8,128)}, f32[160,384]{1,0:T(8,128)}, u32[]{:S(2)}, u32[]{:S(2)}) collective-permute-start(f32[160,384]{1,0:T(8,128)} %add.282), channel_id=1, source_target_pairs={{0,8},{1,9},{2,10},{3,11},{4,36},{5,37},{6,38},{7,39},{8,0},{9,1},... | collective-permute-start | bytes 737288 | tf_op jit(solution)/shard_map/ppermute | solution.py:153
  197.2 18.6 %collective-permute-start.22 = (f32[896,384]{1,0:T(8,128)}, f32[896,384]{1,0:T(8,128)}, u32[]{:S(2)}, u32[]{:S(2)}) collective-permute-start(f32[896,384]{1,0:T(8,128)} %maximum_select_fusion.5), channel_id=1, source_target_pairs={{0,32},{1,33},{2,34},{3,35},{4,12},{5,13},{6,14},{7,15},{8,40},{9,... | collective-permute-start | bytes 4128776 | tf_op jit(solution)/shard_map/ppermute | solution.py:153
  197.6 24.5 %collective-permute-start.10 = (f32[512,768]{1,0:T(8,128)S(1)}, f32[512,768]{1,0:T(8,128)}, u32[]{:S(2)}, u32[]{:S(2)}) collective-permute-start(f32[512,768]{1,0:T(8,128)S(1)} %dynamic-slice_add_fusion), channel_id=1, source_target_pairs={{0,3},{1,2},{2,1},{3,0},{4,5},{5,4},{6,7},{7,6},{8,11},{9,10},{10,... | collective-permute-start | bytes 4718600 | tf_op jit(solution)/shard_map/ppermute | solution.py:153
  199.1 6.4 %collective-permute-start.17 = (f32[160,384]{1,0:T(8,128)}, f32[160,384]{1,0:T(8,128)S(1)}, u32[]{:S(2)}, u32[]{:S(2)}) collective-permute-start(f32[160,384]{1,0:T(8,128)} %add.283), channel_id=1, source_target_pairs={{0,24},{1,25},{2,26},{3,27},{4,100},{5,101},{6,102},{7,103},{8,16}... | collective-permute-start | bytes 737288 | tf_op jit(solution)/shard_map/ppermute | solution.py:153
  206.6 13.6 %collective-permute-start.18 = (f32[320,384]{1,0:T(8,128)S(1)}, f32[320,384]{1,0:T(8,128)}, u32[]{:S(2)}, u32[]{:S(2)}) collective-permute-start(f32[320,384]{1,0:T(8,128)S(1)} %maximum_select_fusion.7), channel_id=1, source_target_pairs={{0,96},{1,97},{2,98},{3,99},{4,28},{5,29},{6,30},{7,31},{8,104},{9... | collective-permute-start | bytes 1474568 | tf_op jit(solution)/shard_map/ppermute | solution.py:153
  220.2 32.1 %collective-permute-start.23 = (f32[1792,384]{1,0:T(8,128)}, f32[1792,384]{1,0:T(8,128)}, u32[]{:S(2)}, u32[]{:S(2)}) collective-permute-start(f32[1792,384]{1,0:T(8,128)} %maximum_select_fusion.3), channel_id=1, source_target_pairs={{0,4},{1,5},{2,6},{3,7},{4,0},{5,1},{6,2},{7,3},{8,12},{9,13},{10,... | collective-permute-start | bytes 8257544 | tf_op jit(solution)/shard_map/ppermute | solution.py:153
  221.5 5.2 %collective-permute-start.19 = (f32[640,384]{1,0:T(8,128)S(1)}, f32[640,384]{1,0:T(8,128)S(1)}, u32[]{:S(2)}, u32[]{:S(2)}) collective-permute-start(f32[640,384]{1,0:T(8,128)S(1)} %maximum_select_fusion.6), channel_id=1, source_target_pairs={{0,4},{1,5},{2,6},{3,7},{4,0},{5,1},{6,2},{7,3},{8,12},{9,13},{10,... | collective-permute-start | bytes 2949128 | tf_op jit(solution)/shard_map/ppermute | solution.py:153
  223.7 26.8 %collective-permute-start.16 = (f32[512,768]{1,0:T(8,128)S(1)}, f32[512,768]{1,0:T(8,128)S(1)}, u32[]{:S(2)}, u32[]{:S(2)}) collective-permute-start(f32[512,768]{1,0:T(8,128)S(1)} %add.284), channel_id=1, source_target_pairs={{0,1},{1,0},{2,3},{3,2},{4,7},{5,6},{6,5},{7,4},{8,9},{9,8},{10,11... | collective-permute-start | bytes 4718600 | tf_op jit(solution)/shard_map/ppermute | solution.py:153
  226.9 17.9 %collective-permute-start.20 = (f32[8,768]{1,0:T(8,128)S(1)}, f32[8,768]{1,0:T(8,128)S(1)}, u32[]{:S(2)}, u32[]{:S(2)}) collective-permute-start(f32[8,768]{1,0:T(8,128)S(1)} %slice.282), channel_id=1, source_target_pairs={{0,1},{1,0},{2,3},{3,2},{4,5},{5,4},{6,7},{7,6},{8,9},{9,8},{10,11... | collective-permute-start | bytes 73736 | tf_op jit(solution)/shard_map/ppermute | solution.py:153
  244.8 5.0 %collective-permute-start.21 = (f32[8,768]{1,0:T(8,128)S(1)}, f32[8,768]{1,0:T(8,128)S(1)}, u32[]{:S(2)}, u32[]{:S(2)}) collective-permute-start(f32[8,768]{1,0:T(8,128)S(1)} %slice_add_fusion), channel_id=1, source_target_pairs={{0,3},{1,2},{2,1},{3,0},{4,7},{5,6},{6,5},{7,4},{8,11},{9,10},{10,... | collective-permute-start | bytes 73736 | tf_op jit(solution)/shard_map/ppermute | solution.py:153
  (69 other events, 326.0 us)

commit v2 on v1

--- a/solution.py
+++ b/solution.py
@@ -339,10 +339,9 @@
     early_other = early_columns(1 - core)
     early_own = early_columns(core)
     early = Exchange(early_phases, 3, "dp").put_halves(early_own, early_other)
-    landed = [out.land(early_own)]
 
     context_grad = jnp.dot(
-        after(cotangent, landed), dense_weight.T, preferred_element_type=jnp.float32
+        after(cotangent, early_own), dense_weight.T, preferred_element_type=jnp.float32
     ).astype(jnp.bfloat16)
     context_grad = context_grad.reshape(row_count, head_count, HD).transpose(1, 0, 2)
     landed = [early.land(context_grad)]
@@ -357,8 +356,14 @@
         row_count, columns
     )
     mixed_low = mixed_grad.astype(jnp.bfloat16)
-    first_up = jnp.dot(mixed_low, heads_weight.T, preferred_element_type=jnp.float32)
-    second_up = jnp.dot(pre_low, expand_weight.T, preferred_element_type=jnp.float32)
+    landed = early.land(mixed_low)
+    first_up = jnp.dot(
+        after(mixed_low, landed), heads_weight.T, preferred_element_type=jnp.float32
+    )
+    landed = out.land(first_up)
+    second_up = jnp.dot(
+        after(pre_low, landed), expand_weight.T, preferred_element_type=jnp.float32
+    )
     input_part = norm_backward(first_up, normed, norm_scale, first_gain) + norm_backward(
         second_up, normed, norm_scale, second_gain
     )
@@ -391,12 +396,14 @@
     landed = early.land(landed)
     landed = back.land(landed)
     landed = late.land(landed)
+    landed = late.land(landed)
     landed = early.land(landed)
     landed = late.land(landed)
     landed = late.land(landed)
+    landed = back.land(landed)
+    landed = late.land(landed)
     landed = early.land(landed)
-    landed = back.land(landed)
-    landed = late.finish()
+    late.finish()
     early.finish()
     back.finish()
 

time: 267 us -> 259 us (0.970)
  the two profiles are of different devices: /device:TPU:64 before, /device:TPU:0 now
where the time goes in v2:
time: 259 us; the launch traced here: 254 us
  waiting for transfers between devices  79.3 us (31%)
  other arithmetic  54.6 us (21%)
  matrix products  53.3 us (21%)
  starting transfers between devices  39.9 us (15%)
  local copies, waits for them, and re-layouts  24.9 us (10%)
    ppermute x24, waiting for transfers between devices, swap(): return lax.ppermute(values, ('dp', 'tensor'), pairs)  79.3 us
    ppermute x24, starting transfers between devices, swap(): return lax.ppermute(values, ('dp', 'tensor'), pairs)  39.9 us
    dot_general x12, matrix products, contract(): jnp.einsum(pattern, left_op, right_op, preferred_element_type=jnp.float32)  17.8 us
    add x14, other arithmetic, land(): self.values = self.values + arrived  17.7 us
    unnamed x143, local copies, waits for them, and re-layouts  9.69 us
    select_n x6, other arithmetic, joined(): jnp.where(which == 0, jnp.concatenate([own, other], axis=axis), jnp.conca...  9.41 us
    dot_general x4, matrix products, early_columns(): jnp.dot(left.T, half_of(right, which, 1), preferred_element_type=jnp.floa...  6.68 us
    dot_general x2, matrix products, late_columns(): jnp.dot(mixed_low.T, half_of(first_input, which, 1), preferred_element_ty...  5.58 us
  transfers between devices with their start and end apart: 24, of which 13 were waited for; matrix products, arithmetic and copies ran while one was open for 23% of the time, Pallas kernels for 0%

profile of v2, /device:TPU:0, one launch (start us, length us, event | category | flops | bytes accessed | tf_op | source)
XLA Modules:
  0.0 254.0 jit_solution(14705209344482677943)
XLA Ops:
  23.5 3.9 %fusion.60 = bf16[3,512,64]{1,2,0:T(8,128)(2,1)} fusion(f32[3,512,1024]{2,1,0:T(8,128)S(1)} %get-tuple-element.186, f32[3,512]{1,0:T(4,128)S(1)} %fusion, f32[3,512]{1,0:T(4,128)S(1)} %get-tuple-element.185, pred[512,1024]{1,0:T(8,128)(4,1)S(1)} %fusion.43, f32[1024,3,3,64]{0,3,2,1:T(8,128)} %bitcast.68), kind=kOutput, calls=%fused_computation.91 | convolution fusion | flops 209289216 | bytes 7417856 | tf_op jit(solution)/shard_map/hqk,hkd->hqd/dot_general | solution.py:18
  31.8 3.1 %multiply_convert_fusion.2 = (bf16[1024,768]{0,1:T(8,128)(2,1)S(1)}, f32[1024,768]{0,1:T(8,128)}) fusion(f32[768]{0:T(1024)S(1)} %copy-done.63, bf16[1024,768]{1,0:T(8,128)(2,1)S(1)} %copy-done.22, bf16[768,768]{1,0:T(8,128)(2,1)S(1)} %copy-done), kind=kOutput, calls=%fused_computation.51 | convolution fusion | flops 1212678144 | bytes 7474176 | tf_op jit(solution)/shard_map/dot_general | solution.py:303
  38.1 5.1 %fusion.34 = bf16[1024,768]{0,1:T(8,128)(2,1)S(1)} fusion(f32[1024,768]{0,1:T(8,128)} %get-tuple-element.190, bf16[1024,768]{1,0:T(8,128)(2,1)} %param.43, bf16[768,768]{1,0:T(8,128)(2,1)} %param.41, f32[768]{0:T(1024)} %param.40), kind=kOutput, calls=%fused_computation.44 | convolution fusion | flops 1216610304 | bytes 7474176 | tf_op jit(solution)/shard_map/dot_general | solution.py:322
  49.7 3.5 %convolution_add_fusion.1 = f32[512,768]{1,0:T(8,128)} fusion(f32[512,768]{1,0:T(8,128)S(1)} %fusion.83, bf16[768,768]{1,0:T(8,128)(2,1)} %param.41, bf16[1024,768]{0,1:T(8,128)(2,1)} %copy-done.64, s32[]{:T(128)S(6)} %select_n.137), kind=kOutput, calls=%fused_computation.82 | convolution fusion | flops 604372992 | bytes 5111812 | tf_op jit(solution)/shard_map/dot_general | solution.py:313
  66.8 3.9 %multiply_convert_fusion = bf16[3,512,1024]{2,1,0:T(8,128)(2,1)S(1)} fusion(f32[3,512,1024]{2,1,0:T(8,128)S(1)} %bitcast.62, f32[3,512]{1,0:T(4,128)S(1)} %get-tuple-element.143, f32[3,512]{1,0:T(4,128)S(1)} %log_add_fusion, pred[512,1024]{1,0:T(8,128)(4,1)S(1)} %copy-done.15, bf16[3,1024,64]{1,2,0:T(8,128)(2,1)S(1)} %bitcast.72, f32[1024,3,3,64]{0,3,2,1:T(8,128)} %bitcast.69), kind=kOutput, calls=%fused_computation | convolution fusion | flops 212336640 | bytes 10567680 | tf_op jit(solution)/shard_map/hqd,hkd->hqk/dot_general | solution.py:18
  79.5 3.1 %collective-permute-start.2 = (f32[512,768]{1,0:T(8,128)}, f32[512,768]{1,0:T(8,128)}, u32[]{:S(2)}, u32[]{:S(2)}) collective-permute-start(f32[512,768]{1,0:T(8,128)} %add.257), channel_id=1, source_target_pairs={{0,3},{1,2},{2,1},{3,0},{4,5},{5,4},{6,7},{7,6},{8,11},{9,10},{10,... | collective-permute-start | bytes 4718600 | tf_op jit(solution)/shard_map/ppermute | solution.py:153
  85.1 9.8 %collective-permute-done.3 = f32[896,384]{1,0:T(8,128)S(1)} collective-permute-done((f32[896,384]{1,0:T(8,128)S(1)}, f32[896,384]{1,0:T(8,128)S(1)}, u32[]{:S(2)}, u32[]{:S(2)}) %collective-permute-start.3) | collective-permute-done | bytes 1376288 | tf_op jit(solution)/shard_map/ppermute | solution.py:153
  100.6 3.3 %fusion.68 = f32[576,384]{1,0:T(8,128)} fusion(bf16[1024,576]{0,1:T(8,128)(2,1)} %bitcast.79, bf16[1024,768]{1,0:T(8,128)(2,1)} %copy-done.21, s32[]{:T(128)S(6)} %select_n.139), kind=kOutput, calls=%fused_computation.109 | convolution fusion | flops 452984832 | bytes 2850820 | tf_op jit(solution)/shard_map/dot_general | solution.py:384
  103.9 3.8 %collective-permute-done.4 = f32[448,384]{1,0:T(8,128)} collective-permute-done((f32[448,384]{1,0:T(8,128)S(1)}, f32[448,384]{1,0:T(8,128)}, u32[]{:S(2)}, u32[]{:S(2)}) %collective-permute-start.4) | collective-permute-done | bytes 688160 | tf_op jit(solution)/shard_map/ppermute | solution.py:153
  110.6 4.4 %add.265 = f32[512,768]{1,0:T(8,128)} add(f32[512,768]{1,0:T(8,128)} %add.257, f32[512,768]{1,0:T(8,128)} %collective-permute-done.2) | non-fusion elementwise | flops 393216 | bytes 4718592 | tf_op jit(solution)/shard_map/add | solution.py:241
  116.7 4.6 %fusion.23 = (f32[1024]{0:T(1024)S(1)}, f32[768]{0:T(1024)S(1)}, f32[1024]{0:T(1024)S(1)}, f32[768]{0:T(1024)S(1)}, f32[768]{0:T(1024)S(1)}, /*index=5*/f32[1024...) fusion(bf16[1024,768]{1,0:T(8,128)(2,1)S(1)} %copy-done.3, f32[768]{0:T(1024)S(1)} %copy-done.46, ...), kind=kOutput, calls=%fused_computation.33 | convolution fusion | flops 1221321728 | bytes 10659840 | tf_op jit(solution)/shard_map/dot_general | solution.py:364
  128.1 9.4 %collective-permute-done.7 = f32[448,384]{1,0:T(8,128)S(1)} collective-permute-done((f32[448,384]{1,0:T(8,128)S(1)}, f32[448,384]{1,0:T(8,128)S(1)}, u32[]{:S(2)}, u32[]{:S(2)}) %collective-permute-start.7) | collective-permute-done | bytes 688160 | tf_op jit(solution)/shard_map/ppermute | solution.py:153
  141.2 5.5 %fusion.28 = (bf16[1024,768]{1,0:T(8,128)(2,1)}, f32[1024,768]{1,0:T(8,128)S(1)}) fusion(bf16[1024,768]{1,0:T(8,128)(2,1)S(1)} %copy-done.3, f32[768]{0:T(1024)S(1)} %copy-done.53, f32[768]{0:T(1024)S(1)} %copy-done.54, f32[512,768]{1,0:T(8,128)} %add.265, f32[512,768]{1,0:T(8,128)} %collective-permute-done.5, pred[]{:T(512)S(6)} %eq.86, ...), kind=kLoop, calls=%fused_computation.38 | loop fusion | flops 15728640 | bytes 15765505 | tf_op jit(solution)/shard_map/convert_element_type | solution.py:410
  149.7 4.1 %collective-permute-start.9 = (f32[448,384]{1,0:T(8,128)S(1)}, f32[448,384]{1,0:T(8,128)}, u32[]{:S(2)}, u32[]{:S(2)}) collective-permute-start(f32[448,384]{1,0:T(8,128)S(1)} %add.266), channel_id=1, source_target_pairs={{0,24},{1,25},{2,26},{3,27},{4,100},{5,101},{6,102},{7,103},{8,16}... | collective-permute-start | bytes 2064392 | tf_op jit(solution)/shard_map/ppermute | solution.py:153
  156.6 11.5 %collective-permute-done.10 = f32[320,384]{1,0:T(8,128)S(1)} collective-permute-done((f32[320,384]{1,0:T(8,128)}, f32[320,384]{1,0:T(8,128)S(1)}, u32[]{:S(2)}, u32[]{:S(2)}) %collective-permute-start.10) | collective-permute-done | bytes 491552 | tf_op jit(solution)/shard_map/ppermute | solution.py:153
  174.2 3.6 %collective-permute-done.12 = f32[160,384]{1,0:T(8,128)S(1)} collective-permute-done((f32[160,384]{1,0:T(8,128)S(1)}, f32[160,384]{1,0:T(8,128)S(1)}, u32[]{:S(2)}, u32[]{:S(2)}) %collective-permute-start.12) | collective-permute-done | bytes 245792 | tf_op jit(solution)/shard_map/ppermute | solution.py:153
  180.9 3.2 %collective-permute-done.13 = f32[160,384]{1,0:T(8,128)S(1)} collective-permute-done((f32[160,384]{1,0:T(8,128)S(1)}, f32[160,384]{1,0:T(8,128)S(1)}, u32[]{:S(2)}, u32[]{:S(2)}) %collective-permute-start.13) | collective-permute-done | bytes 245792 | tf_op jit(solution)/shard_map/ppermute | solution.py:153
  184.2 3.2 %maximum_select_fusion.5 = f32[896,384]{1,0:T(8,128)} fusion(f32[448,384]{1,0:T(8,128)} %collective-permute-done.15, f32[448,384]{1,0:T(8,128)} %add.278, pred[]{:T(512)S(6)} %eq.96), kind=kLoop, calls=%fused_computation.84 | loop fusion | flops 1032192 | bytes 2752513 | tf_op jit(solution)/shard_map/jit(_where)/select_n | solution.py:162
  188.4 7.8 %collective-permute-done.14 = f32[160,384]{1,0:T(8,128)S(1)} collective-permute-done((f32[160,384]{1,0:T(8,128)S(1)}, f32[160,384]{1,0:T(8,128)S(1)}, u32[]{:S(2)}, u32[]{:S(2)}) %collective-permute-start.14) | collective-permute-done | bytes 245792 | tf_op jit(solution)/shard_map/ppermute | solution.py:153
  199.1 4.7 %collective-permute-done.16 = f32[160,384]{1,0:T(8,128)} collective-permute-done((f32[160,384]{1,0:T(8,128)S(1)}, f32[160,384]{1,0:T(8,128)}, u32[]{:S(2)}, u32[]{:S(2)}) %collective-permute-start.16) | collective-permute-done | bytes 245792 | tf_op jit(solution)/shard_map/ppermute | solution.py:153
  209.5 5.9 %collective-permute-done.18 = f32[320,384]{1,0:T(8,128)} collective-permute-done((f32[320,384]{1,0:T(8,128)S(1)}, f32[320,384]{1,0:T(8,128)}, u32[]{:S(2)}, u32[]{:S(2)}) %collective-permute-start.18) | collective-permute-done | bytes 491552 | tf_op jit(solution)/shard_map/ppermute | solution.py:153
  216.6 3.0 %maximum_select_fusion.3 = f32[1792,384]{1,0:T(8,128)S(1)} fusion(f32[896,384]{1,0:T(8,128)} %collective-permute-done.22, f32[896,384]{1,0:T(8,128)} %maximum_select_fusion.5, pred[]{:T(512)S(6)} %eq.98), kind=kLoop, calls=%fused_computation.65 | loop fusion | flops 2064384 | bytes 5505025 | tf_op jit(solution)/shard_map/jit(_where)/select_n | solution.py:162
  221.8 4.4 %collective-permute-done.19 = f32[640,384]{1,0:T(8,128)S(1)} collective-permute-done((f32[640,384]{1,0:T(8,128)S(1)}, f32[640,384]{1,0:T(8,128)S(1)}, u32[]{:S(2)}, u32[]{:S(2)}) %collective-permute-start.19) | collective-permute-done | bytes 983072 | tf_op jit(solution)/shard_map/ppermute | solution.py:153
  229.5 11.7 %collective-permute-done.20 = f32[8,768]{1,0:T(8,128)S(1)} collective-permute-done((f32[8,768]{1,0:T(8,128)S(1)}, f32[8,768]{1,0:T(8,128)S(1)}, u32[]{:S(2)}, u32[]{:S(2)}) %collective-permute-start.20) | collective-permute-done | bytes 24608 | tf_op jit(solution)/shard_map/ppermute | solution.py:153
  (293 shorter events, 125.3 us)
Async XLA Ops:
  48.1 13.1 %collective-permute-start.1 = (f32[1792,384]{1,0:T(8,128)}, f32[1792,384]{1,0:T(8,128)}, u32[]{:S(2)}, u32[]{:S(2)}) collective-permute-start(f32[1792,384]{1,0:T(8,128)} %pad_maximum_fusion.1), channel_id=1, source_target_pairs={{0,4},{1,5},{2,6},{3,7},{4,0},{5,1},{6,2},{7,3},{8,12},{9,13},{10,... | collective-permute-start | bytes 8257544 | tf_op jit(solution)/shard_map/ppermute | solution.py:153
  53.2 20.7 %collective-permute-start = (f32[512,768]{1,0:T(8,128)}, f32[512,768]{1,0:T(8,128)}, u32[]{:S(2)}, u32[]{:S(2)}) collective-permute-start(f32[512,768]{1,0:T(8,128)} %convolution_add_fusion.1), channel_id=1, source_target_pairs={{0,1},{1,0},{2,3},{3,2},{4,7},{5,6},{6,5},{7,4},{8,9},{9,8},{10,11... | collective-permute-start | bytes 4718600 | tf_op jit(solution)/shard_map/ppermute | solution.py:153
  76.6 18.3 %collective-permute-start.3 = (f32[896,384]{1,0:T(8,128)S(1)}, f32[896,384]{1,0:T(8,128)S(1)}, u32[]{:S(2)}, u32[]{:S(2)}) collective-permute-start(f32[896,384]{1,0:T(8,128)S(1)} %get-tuple-element.152), channel_id=1, source_target_pairs={{0,32},{1,33},{2,34},{3,35},{4,12},{5,13},{6,14},{7,15},{8,40},{9,... | collective-permute-start | bytes 4128776 | tf_op jit(solution)/shard_map/ppermute | solution.py:153
  79.5 31.1 %collective-permute-start.2 = (f32[512,768]{1,0:T(8,128)}, f32[512,768]{1,0:T(8,128)}, u32[]{:S(2)}, u32[]{:S(2)}) collective-permute-start(f32[512,768]{1,0:T(8,128)} %add.257), channel_id=1, source_target_pairs={{0,3},{1,2},{2,1},{3,0},{4,5},{5,4},{6,7},{7,6},{8,11},{9,10},{10,... | collective-permute-start | bytes 4718600 | tf_op jit(solution)/shard_map/ppermute | solution.py:153
  96.2 11.5 %collective-permute-start.4 = (f32[448,384]{1,0:T(8,128)S(1)}, f32[448,384]{1,0:T(8,128)}, u32[]{:S(2)}, u32[]{:S(2)}) collective-permute-start(f32[448,384]{1,0:T(8,128)S(1)} %get-tuple-element.159), channel_id=1, source_target_pairs={{0,8},{1,9},{2,10},{3,11},{4,36},{5,37},{6,38},{7,39},{8,0},{9,1},... | collective-permute-start | bytes 2064392 | tf_op jit(solution)/shard_map/ppermute | solution.py:153
  115.0 24.9 %collective-permute-start.5 = (f32[512,768]{1,0:T(8,128)}, f32[512,768]{1,0:T(8,128)}, u32[]{:S(2)}, u32[]{:S(2)}) collective-permute-start(f32[512,768]{1,0:T(8,128)} %add.265), channel_id=1, source_target_pairs={{0,1},{1,0},{2,3},{3,2},{4,7},{5,6},{6,5},{7,4},{8,9},{9,8},{10,11... | collective-permute-start | bytes 4718600 | tf_op jit(solution)/shard_map/ppermute | solution.py:153
  122.6 16.2 %collective-permute-start.6 = (f32[640,384]{1,0:T(8,128)S(1)}, f32[640,384]{1,0:T(8,128)S(1)}, u32[]{:S(2)}, u32[]{:S(2)}) collective-permute-start(f32[640,384]{1,0:T(8,128)S(1)} %pad_maximum_fusion.7), channel_id=1, source_target_pairs={{0,4},{1,5},{2,6},{3,7},{4,0},{5,1},{6,2},{7,3},{8,12},{9,13},{10,... | collective-permute-start | bytes 2949128 | tf_op jit(solution)/shard_map/ppermute | solution.py:153
  125.2 12.2 %collective-permute-start.7 = (f32[448,384]{1,0:T(8,128)S(1)}, f32[448,384]{1,0:T(8,128)S(1)}, u32[]{:S(2)}, u32[]{:S(2)}) collective-permute-start(f32[448,384]{1,0:T(8,128)S(1)} %add.264), channel_id=1, source_target_pairs={{0,96},{1,97},{2,98},{3,99},{4,28},{5,29},{6,30},{7,31},{8,104},{9... | collective-permute-start | bytes 2064392 | tf_op jit(solution)/shard_map/ppermute | solution.py:153
  149.6 23.0 %collective-permute-start.8 = (f32[512,768]{1,0:T(8,128)}, f32[512,768]{1,0:T(8,128)}, u32[]{:S(2)}, u32[]{:S(2)}) collective-permute-start(f32[512,768]{1,0:T(8,128)} %constant_dynamic-slice_fusion.3), channel_id=1, source_target_pairs={{0,1},{1,0},{2,3},{3,2},{4,7},{5,6},{6,5},{7,4},{8,9},{9,8},{10,11... | collective-permute-start | bytes 4718600 | tf_op jit(solution)/shard_map/ppermute | solution.py:153
  149.7 18.5 %collective-permute-start.9 = (f32[448,384]{1,0:T(8,128)S(1)}, f32[448,384]{1,0:T(8,128)}, u32[]{:S(2)}, u32[]{:S(2)}) collective-permute-start(f32[448,384]{1,0:T(8,128)S(1)} %add.266), channel_id=1, source_target_pairs={{0,24},{1,25},{2,26},{3,27},{4,100},{5,101},{6,102},{7,103},{8,16}... | collective-permute-start | bytes 2064392 | tf_op jit(solution)/shard_map/ppermute | solution.py:153
  153.8 14.3 %collective-permute-start.10 = (f32[320,384]{1,0:T(8,128)}, f32[320,384]{1,0:T(8,128)S(1)}, u32[]{:S(2)}, u32[]{:S(2)}) collective-permute-start(f32[320,384]{1,0:T(8,128)} %get-tuple-element.161), channel_id=1, source_target_pairs={{0,96},{1,97},{2,98},{3,99},{4,28},{5,29},{6,30},{7,31},{8,104},{9... | collective-permute-start | bytes 1474568 | tf_op jit(solution)/shard_map/ppermute | solution.py:153
  170.2 13.9 %collective-permute-start.15 = (f32[448,384]{1,0:T(8,128)}, f32[448,384]{1,0:T(8,128)}, u32[]{:S(2)}, u32[]{:S(2)}) collective-permute-start(f32[448,384]{1,0:T(8,128)} %add.278), channel_id=1, source_target_pairs={{0,8},{1,9},{2,10},{3,11},{4,36},{5,37},{6,38},{7,39},{8,0},{9,1},... | collective-permute-start | bytes 2064392 | tf_op jit(solution)/shard_map/ppermute | solution.py:153
  170.4 7.4 %collective-permute-start.12 = (f32[160,384]{1,0:T(8,128)S(1)}, f32[160,384]{1,0:T(8,128)S(1)}, u32[]{:S(2)}, u32[]{:S(2)}) collective-permute-start(f32[160,384]{1,0:T(8,128)S(1)} %get-tuple-element.167), channel_id=1, source_target_pairs={{0,24},{1,25},{2,26},{3,27},{4,100},{5,101},{6,102},{7,103},{8,16}... | collective-permute-start | bytes 737288 | tf_op jit(solution)/shard_map/ppermute | solution.py:153
  177.9 6.3 %collective-permute-start.13 = (f32[160,384]{1,0:T(8,128)S(1)}, f32[160,384]{1,0:T(8,128)S(1)}, u32[]{:S(2)}, u32[]{:S(2)}) collective-permute-start(f32[160,384]{1,0:T(8,128)S(1)} %add.281), channel_id=1, source_target_pairs={{0,32},{1,33},{2,34},{3,35},{4,12},{5,13},{6,14},{7,15},{8,40},{9,... | collective-permute-start | bytes 737288 | tf_op jit(solution)/shard_map/ppermute | solution.py:153
  178.0 29.9 %collective-permute-start.11 = (f32[512,768]{1,0:T(8,128)S(1)}, f32[512,768]{1,0:T(8,128)}, u32[]{:S(2)}, u32[]{:S(2)}) collective-permute-start(f32[512,768]{1,0:T(8,128)S(1)} %dynamic-slice_add_fusion), channel_id=1, source_target_pairs={{0,3},{1,2},{2,1},{3,0},{4,5},{5,4},{6,7},{7,6},{8,11},{9,10},{10,... | collective-permute-start | bytes 4718600 | tf_op jit(solution)/shard_map/ppermute | solution.py:153
  187.3 29.3 %collective-permute-start.22 = (f32[896,384]{1,0:T(8,128)}, f32[896,384]{1,0:T(8,128)}, u32[]{:S(2)}, u32[]{:S(2)}) collective-permute-start(f32[896,384]{1,0:T(8,128)} %maximum_select_fusion.5), channel_id=1, source_target_pairs={{0,32},{1,33},{2,34},{3,35},{4,12},{5,13},{6,14},{7,15},{8,40},{9,... | collective-permute-start | bytes 4128776 | tf_op jit(solution)/shard_map/ppermute | solution.py:153
  187.4 8.8 %collective-permute-start.14 = (f32[160,384]{1,0:T(8,128)S(1)}, f32[160,384]{1,0:T(8,128)S(1)}, u32[]{:S(2)}, u32[]{:S(2)}) collective-permute-start(f32[160,384]{1,0:T(8,128)S(1)} %add.282), channel_id=1, source_target_pairs={{0,8},{1,9},{2,10},{3,11},{4,36},{5,37},{6,38},{7,39},{8,0},{9,1},... | collective-permute-start | bytes 737288 | tf_op jit(solution)/shard_map/ppermute | solution.py:153
  196.2 7.6 %collective-permute-start.16 = (f32[160,384]{1,0:T(8,128)S(1)}, f32[160,384]{1,0:T(8,128)}, u32[]{:S(2)}, u32[]{:S(2)}) collective-permute-start(f32[160,384]{1,0:T(8,128)S(1)} %add.283), channel_id=1, source_target_pairs={{0,24},{1,25},{2,26},{3,27},{4,100},{5,101},{6,102},{7,103},{8,16}... | collective-permute-start | bytes 737288 | tf_op jit(solution)/shard_map/ppermute | solution.py:153
  205.0 10.4 %collective-permute-start.18 = (f32[320,384]{1,0:T(8,128)S(1)}, f32[320,384]{1,0:T(8,128)}, u32[]{:S(2)}, u32[]{:S(2)}) collective-permute-start(f32[320,384]{1,0:T(8,128)S(1)} %maximum_select_fusion.7), channel_id=1, source_target_pairs={{0,96},{1,97},{2,98},{3,99},{4,28},{5,29},{6,30},{7,31},{8,104},{9... | collective-permute-start | bytes 1474568 | tf_op jit(solution)/shard_map/ppermute | solution.py:153
  219.7 29.0 %collective-permute-start.23 = (f32[1792,384]{1,0:T(8,128)S(1)}, f32[1792,384]{1,0:T(8,128)S(1)}, u32[]{:S(2)}, u32[]{:S(2)}) collective-permute-start(f32[1792,384]{1,0:T(8,128)S(1)} %maximum_select_fusion.3), channel_id=1, source_target_pairs={{0,4},{1,5},{2,6},{3,7},{4,0},{5,1},{6,2},{7,3},{8,12},{9,13},{10,... | collective-permute-start | bytes 8257544 | tf_op jit(solution)/shard_map/ppermute | solution.py:153
  219.8 6.5 %collective-permute-start.19 = (f32[640,384]{1,0:T(8,128)S(1)}, f32[640,384]{1,0:T(8,128)S(1)}, u32[]{:S(2)}, u32[]{:S(2)}) collective-permute-start(f32[640,384]{1,0:T(8,128)S(1)} %maximum_select_fusion.6), channel_id=1, source_target_pairs={{0,4},{1,5},{2,6},{3,7},{4,0},{5,1},{6,2},{7,3},{8,12},{9,13},{10,... | collective-permute-start | bytes 2949128 | tf_op jit(solution)/shard_map/ppermute | solution.py:153
  220.3 26.6 %collective-permute-start.17 = (f32[512,768]{1,0:T(8,128)S(1)}, f32[512,768]{1,0:T(8,128)S(1)}, u32[]{:S(2)}, u32[]{:S(2)}) collective-permute-start(f32[512,768]{1,0:T(8,128)S(1)} %add.284), channel_id=1, source_target_pairs={{0,1},{1,0},{2,3},{3,2},{4,7},{5,6},{6,5},{7,4},{8,9},{9,8},{10,11... | collective-permute-start | bytes 4718600 | tf_op jit(solution)/shard_map/ppermute | solution.py:153
  226.5 14.7 %collective-permute-start.20 = (f32[8,768]{1,0:T(8,128)S(1)}, f32[8,768]{1,0:T(8,128)S(1)}, u32[]{:S(2)}, u32[]{:S(2)}) collective-permute-start(f32[8,768]{1,0:T(8,128)S(1)} %slice.282), channel_id=1, source_target_pairs={{0,1},{1,0},{2,3},{3,2},{4,5},{5,4},{6,7},{7,6},{8,9},{9,8},{10,11... | collective-permute-start | bytes 73736 | tf_op jit(solution)/shard_map/ppermute | solution.py:153
  241.2 5.0 %collective-permute-start.21 = (f32[8,768]{1,0:T(8,128)S(1)}, f32[8,768]{1,0:T(8,128)S(1)}, u32[]{:S(2)}, u32[]{:S(2)}) collective-permute-start(f32[8,768]{1,0:T(8,128)S(1)} %slice_add_fusion), channel_id=1, source_target_pairs={{0,3},{1,2},{2,1},{3,0},{4,7},{5,6},{6,5},{7,4},{8,11},{9,10},{10,... | collective-permute-start | bytes 73736 | tf_op jit(solution)/shard_map/ppermute | solution.py:153
  (71 other events, 344.8 us)
